TPU v7x, 32 devices: a whole 2x2x4 slice. The times are simulated.
32 devices in a mesh: dp: 8 (over z, x), tm: 4 (over y, core).
Axes of the slice: x: 2, y: 2, z: 4, core: 2. Of those that a mesh axis runs over, the one named last changes fastest.
Arguments:
- clips: bfloat16 [8, 32, 16, 16, 256], P('dp', 'tm'), may hold values from -6 to 6
- frame_counts: int32 [8], P('dp'), may hold values from 5 to 32, as said below
- weight: bfloat16 [6912, 256], P('dp'), may hold values from -0.078125 to 0.078125
- gain: float32 [256], replicated, may hold values from 0.1 to 1.9
- bias: float32 [256], replicated, may hold values from -3 to 3
- cotangent: bfloat16 [8, 16, 8, 8, 256], P('dp', 'tm'), may hold values from -6 to 6
Outputs:
- output: bfloat16 [8, 16, 8, 8, 256], P('dp', 'tm')
- input_grad: bfloat16 [8, 32, 16, 16, 256], P('dp', 'tm')
- weight_grad: float32 [6912, 256], P('dp')
Inputs may be any that keep to these rules, and one draw needn't show every extreme that they name: frame_counts[c] frames of clip c are valid, the remaining slots are padding; in every draw some clip uses all 32 slots.
All inputs are finite; a program needn't handle non-finite values.
Results may differ from a plain program's by a relative error of at most 0.0048.
Values may be sent and summed in bfloat16 or wider, within the bound.
A program may use at most 64 MiB of HBM per device.

v0:
```python
import jax
import jax.numpy as jnp
from jax import lax
from jax.sharding import PartitionSpec as P

GROUPS = 32
EPS = 1e-06


def shifted(value, axis, by):
    devices = lax.axis_size(axis)
    pairs = [(i, i + by) for i in range(devices) if 0 <= i + by < devices]
    return lax.ppermute(value, axis, pairs)


def unfold(padded, frames_out, rows_out, cols_out):
    tap_list = []
    for step_t in range(3):
        for step_r in range(3):
            for step_c in range(3):
                tap_piece = padded[
                    step_t : step_t + 2 * frames_out : 2,
                    step_r : step_r + 2 * rows_out : 2,
                    step_c : step_c + 2 * cols_out : 2,
                    :,
                ]
                tap_list.append(tap_piece.reshape(frames_out * rows_out * cols_out, -1))
    return jnp.concatenate(tap_list, axis=1)


def spread_taps(values, data_axis, tap_axis, length):
    moved = jnp.moveaxis(values, tap_axis, 0)
    count = moved.shape[data_axis + 1]
    width_list = [(0, 0)] * (moved.ndim - 1)
    after = list(width_list)
    after[data_axis] = (0, 1)
    before = list(width_list)
    before[data_axis] = (1, 0)
    even_part = jnp.pad(moved[0], after) + jnp.pad(moved[2], before)
    odd_part = jnp.pad(moved[1], after)
    joined = jnp.stack([even_part, odd_part], axis=data_axis + 1)
    shape_new = list(even_part.shape)
    shape_new[data_axis] = 2 * (count + 1)
    joined = joined.reshape(shape_new)
    return lax.slice_in_dim(joined, 0, length, axis=data_axis)


def fold_back(columns, padded_shape, frames_out, rows_out, cols_out):
    channels = padded_shape[3]
    blocks = columns.reshape(frames_out, rows_out, cols_out, 3, 3, 3, channels)
    blocks = spread_taps(blocks, 0, 3, padded_shape[0])
    blocks = spread_taps(blocks, 1, 3, padded_shape[1])
    blocks = spread_taps(blocks, 2, 3, padded_shape[2])
    return blocks


def silu_slope(preact):
    sig = jax.nn.sigmoid(preact)
    return sig * (1.0 + preact * (1.0 - sig))


def shards(clips, frame_counts, weight, gain, bias, cotangent):
    clip_data = clips[0]
    cot_block = cotangent[0]
    frame_count, row_count, col_count, channels = clip_data.shape
    width_g = channels // GROUPS
    first_frame = lax.axis_index("tm") * frame_count
    frame_mask = (first_frame + jnp.arange(frame_count) < frame_counts[0]).astype(jnp.float32)[
        :, None, None, None
    ]
    mask_group = frame_mask[..., None]
    entries = frame_counts[0].astype(jnp.float32) * (row_count * col_count * width_g)
    values = clip_data.astype(jnp.float32).reshape(
        frame_count, row_count, col_count, GROUPS, width_g
    )
    sum_first, sum_second = lax.psum(
        (
            jnp.sum(values * mask_group, axis=(0, 1, 2, 4)),
            jnp.sum(values * values * mask_group, axis=(0, 1, 2, 4)),
        ),
        "tm",
    )
    group_mean = sum_first / entries
    variance = sum_second / entries - group_mean * group_mean
    inv_std = lax.rsqrt(variance + EPS)
    normed_g = (values - group_mean[:, None]) * inv_std[:, None]
    normed = normed_g.reshape(frame_count, row_count, col_count, channels)
    preact = normed * gain + bias
    hidden = (jax.nn.silu(preact) * frame_mask).astype(jnp.bfloat16)
    earlier = shifted(hidden[-2:], "tm", 1)
    padded = jnp.pad(jnp.concatenate([earlier, hidden], axis=0), ((0, 0), (1, 0), (1, 0), (0, 0)))
    frames_out, rows_out, cols_out = (frame_count // 2, row_count // 2, col_count // 2)
    patches = unfold(padded, frames_out, rows_out, cols_out)
    cot_rows = cot_block.reshape(-1, channels)
    full_weight = lax.all_gather(weight, "dp", axis=0, tiled=True)
    out_rows = jnp.dot(patches, full_weight, preferred_element_type=jnp.float32)
    out_block = out_rows.astype(jnp.bfloat16).reshape(frames_out, rows_out, cols_out, channels)
    dcols = lax.dot_general(
        cot_rows, full_weight, (((1,), (1,)), ((), ())), preferred_element_type=jnp.float32
    )
    dpad = fold_back(dcols, padded.shape, frames_out, rows_out, cols_out)
    passed = shifted(dpad[:2, 1:, 1:, :], "tm", -1)
    dlocal = dpad[2:, 1:, 1:, :]
    dhidden = jnp.concatenate([dlocal[:-2], dlocal[-2:] + passed], axis=0)
    dnormed = dhidden * frame_mask * silu_slope(preact) * gain
    grad_norm = dnormed.reshape(frame_count, row_count, col_count, GROUPS, width_g)
    back_first, back_second = lax.psum(
        (jnp.sum(grad_norm, axis=(0, 1, 2, 4)), jnp.sum(grad_norm * normed_g, axis=(0, 1, 2, 4))),
        "tm",
    )
    input_grad = (
        mask_group
        * inv_std[:, None]
        * (grad_norm - back_first[:, None] / entries - normed_g * back_second[:, None] / entries)
    )
    input_grad = input_grad.reshape(frame_count, row_count, col_count, channels).astype(
        jnp.bfloat16
    )
    local_grad = lax.dot_general(
        patches, cot_rows, (((0,), (0,)), ((), ())), preferred_element_type=jnp.float32
    )
    clip_grad = lax.psum(local_grad, "tm")
    weight_grad = lax.psum_scatter(clip_grad, "dp", scatter_dimension=0, tiled=True)
    return (out_block[None], input_grad[None], weight_grad)


def solution(mesh):
    placed = (
        P("dp", "tm", None, None, None),
        P("dp"),
        P("dp", None),
        P(),
        P(),
        P("dp", "tm", None, None, None),
    )
    return jax.shard_map(
        shards,
        mesh=mesh,
        in_specs=placed,
        out_specs=(P("dp", "tm", None, None, None), P("dp", "tm", None, None, None), P("dp", None)),
        check_vma=False,
    )
```

profile of v0, /device:TPU:0, one launch (start us, length us, event | category | flops | bytes accessed | tf_op | source)
XLA Modules:
  0.0 398.6 jit_solution(1808083092063788715)
XLA Ops:
  7.2 0.7 all-gather.2.cloned.1.call-update
  8.6 1.8 fusion.18
  10.9 8.4 %all-reduce.11 = (f32[32]{0:T(128)S(1)}, f32[32]{0:T(128)S(1)}) all-reduce(f32[32]{0:T(128)S(1)} %reduce_sum.51, f32[32]{0:T(128)S(1)} %reduce_sum.54), channel_id=1, replica_groups=mesh['dp'=8,'tm'=4] {'tm'}, use_global_device_ids=true, to_apply=%region_2.0 | all-reduce | flops 64 | bytes 512 | tf_op jit(solution)/shard_map/psum | solution.py:76
  19.6 2.1 fusion.15
  21.7 1.3 collective-permute-start
  23.0 1.1 collective-permute-done
  24.2 1.0 fusion.38
  25.2 1.2 slice.155
  26.4 1.2 slice.154
  27.6 0.9 slice.153
  28.5 0.8 slice.152
  29.3 0.8 slice.151
  30.1 0.9 slice.150
  31.0 0.8 slice.149
  31.8 0.8 slice.148
  32.6 1.5 slice.147
  34.1 9.8 %slice.146 = bf16[4,8,8,256]{3,2,1,0:T(8,128)(2,1)} slice(bf16[10,17,17,256]{3,2,1,0:T(8,128)(2,1)S(1)} %fusion.38), slice={[1:9:2], [2:17:2], [1:17:2], [0:256:1]} | slice | bytes 262144 | tf_op jit(solution)/shard_map/slice | solution.py:21
  43.9 9.7 %slice.145 = bf16[4,8,8,256]{3,2,1,0:T(8,128)(2,1)} slice(bf16[10,17,17,256]{3,2,1,0:T(8,128)(2,1)S(1)} %fusion.38), slice={[1:9:2], [2:17:2], [0:16:2], [0:256:1]} | slice | bytes 262144 | tf_op jit(solution)/shard_map/slice | solution.py:21
  53.6 9.8 %slice.144 = bf16[4,8,8,256]{3,2,1,0:T(8,128)(2,1)} slice(bf16[10,17,17,256]{3,2,1,0:T(8,128)(2,1)S(1)} %fusion.38), slice={[1:9:2], [1:17:2], [2:17:2], [0:256:1]} | slice | bytes 262144 | tf_op jit(solution)/shard_map/slice | solution.py:21
  63.4 9.7 %slice.143 = bf16[4,8,8,256]{3,2,1,0:T(8,128)(2,1)} slice(bf16[10,17,17,256]{3,2,1,0:T(8,128)(2,1)S(1)} %fusion.38), slice={[1:9:2], [1:17:2], [1:17:2], [0:256:1]} | slice | bytes 262144 | tf_op jit(solution)/shard_map/slice | solution.py:21
  73.1 9.7 %slice.142 = bf16[4,8,8,256]{3,2,1,0:T(8,128)(2,1)} slice(bf16[10,17,17,256]{3,2,1,0:T(8,128)(2,1)S(1)} %fusion.38), slice={[1:9:2], [1:17:2], [0:16:2], [0:256:1]} | slice | bytes 262144 | tf_op jit(solution)/shard_map/slice | solution.py:21
  82.8 9.7 %slice.141 = bf16[4,8,8,256]{3,2,1,0:T(8,128)(2,1)} slice(bf16[10,17,17,256]{3,2,1,0:T(8,128)(2,1)S(1)} %fusion.38), slice={[1:9:2], [0:16:2], [2:17:2], [0:256:1]} | slice | bytes 262144 | tf_op jit(solution)/shard_map/slice | solution.py:21
  92.5 9.7 %slice.140 = bf16[4,8,8,256]{3,2,1,0:T(8,128)(2,1)} slice(bf16[10,17,17,256]{3,2,1,0:T(8,128)(2,1)S(1)} %fusion.38), slice={[1:9:2], [0:16:2], [1:17:2], [0:256:1]} | slice | bytes 262144 | tf_op jit(solution)/shard_map/slice | solution.py:21
  102.2 9.7 %slice.139 = bf16[4,8,8,256]{3,2,1,0:T(8,128)(2,1)} slice(bf16[10,17,17,256]{3,2,1,0:T(8,128)(2,1)S(1)} %fusion.38), slice={[1:9:2], [0:16:2], [0:16:2], [0:256:1]} | slice | bytes 262144 | tf_op jit(solution)/shard_map/slice | solution.py:21
  111.9 9.8 %slice.138 = bf16[4,8,8,256]{3,2,1,0:T(8,128)(2,1)} slice(bf16[10,17,17,256]{3,2,1,0:T(8,128)(2,1)S(1)} %fusion.38), slice={[0:8:2], [2:17:2], [2:17:2], [0:256:1]} | slice | bytes 262144 | tf_op jit(solution)/shard_map/slice | solution.py:21
  121.7 9.7 %slice.137 = bf16[4,8,8,256]{3,2,1,0:T(8,128)(2,1)} slice(bf16[10,17,17,256]{3,2,1,0:T(8,128)(2,1)S(1)} %fusion.38), slice={[0:8:2], [2:17:2], [1:17:2], [0:256:1]} | slice | bytes 262144 | tf_op jit(solution)/shard_map/slice | solution.py:21
  131.4 9.7 %slice.136 = bf16[4,8,8,256]{3,2,1,0:T(8,128)(2,1)} slice(bf16[10,17,17,256]{3,2,1,0:T(8,128)(2,1)S(1)} %fusion.38), slice={[0:8:2], [2:17:2], [0:16:2], [0:256:1]} | slice | bytes 262144 | tf_op jit(solution)/shard_map/slice | solution.py:21
  141.1 9.8 %slice.135 = bf16[4,8,8,256]{3,2,1,0:T(8,128)(2,1)} slice(bf16[10,17,17,256]{3,2,1,0:T(8,128)(2,1)S(1)} %fusion.38), slice={[0:8:2], [1:17:2], [2:17:2], [0:256:1]} | slice | bytes 262144 | tf_op jit(solution)/shard_map/slice | solution.py:21
  150.9 9.7 %slice.134 = bf16[4,8,8,256]{3,2,1,0:T(8,128)(2,1)} slice(bf16[10,17,17,256]{3,2,1,0:T(8,128)(2,1)S(1)} %fusion.38), slice={[0:8:2], [1:17:2], [1:17:2], [0:256:1]} | slice | bytes 262144 | tf_op jit(solution)/shard_map/slice | solution.py:21
  160.6 9.7 %slice.133 = bf16[4,8,8,256]{3,2,1,0:T(8,128)(2,1)} slice(bf16[10,17,17,256]{3,2,1,0:T(8,128)(2,1)S(1)} %fusion.38), slice={[0:8:2], [1:17:2], [0:16:2], [0:256:1]} | slice | bytes 262144 | tf_op jit(solution)/shard_map/slice | solution.py:21
  170.3 9.8 %slice.132 = bf16[4,8,8,256]{3,2,1,0:T(8,128)(2,1)} slice(bf16[10,17,17,256]{3,2,1,0:T(8,128)(2,1)S(1)} %fusion.38), slice={[0:8:2], [0:16:2], [2:17:2], [0:256:1]} | slice | bytes 262144 | tf_op jit(solution)/shard_map/slice | solution.py:21
  180.1 9.7 %slice.131 = bf16[4,8,8,256]{3,2,1,0:T(8,128)(2,1)} slice(bf16[10,17,17,256]{3,2,1,0:T(8,128)(2,1)S(1)} %fusion.38), slice={[0:8:2], [0:16:2], [1:17:2], [0:256:1]} | slice | bytes 262144 | tf_op jit(solution)/shard_map/slice | solution.py:21
  189.8 9.7 %slice.130 = bf16[4,8,8,256]{3,2,1,0:T(8,128)(2,1)} slice(bf16[10,17,17,256]{3,2,1,0:T(8,128)(2,1)S(1)} %fusion.38), slice={[0:8:2], [0:16:2], [0:16:2], [0:256:1]} | slice | bytes 262144 | tf_op jit(solution)/shard_map/slice | solution.py:21
  199.6 1.5 slice.156
  201.1 1.0 constant_dynamic-update-slice_fusion.26
  202.1 0.9 constant_dynamic-update-slice_fusion.25
  203.0 0.9 constant_dynamic-update-slice_fusion.24
  203.9 0.9 constant_dynamic-update-slice_fusion.23
  204.8 0.9 constant_dynamic-update-slice_fusion.22
  205.8 0.9 constant_dynamic-update-slice_fusion.21
  206.7 0.9 constant_dynamic-update-slice_fusion.20
  207.6 0.9 constant_dynamic-update-slice_fusion.19
  208.5 0.9 constant_dynamic-update-slice_fusion.18
  209.4 0.9 constant_dynamic-update-slice_fusion.17
  210.4 0.9 constant_dynamic-update-slice_fusion.16
  211.3 0.9 constant_dynamic-update-slice_fusion.15
  212.5 1.7 copy-done.3
  214.3 4.1 %fusion.43 = f32[6912,256]{1,0:T(8,128)} fusion(bf16[256,6912]{1,0:T(8,128)(2,1)S(1)} %constant_dynamic-update-slice_fusion, bf16[256,256]{1,0:T(8,128)(2,1)S(1)} %bitcast.127), kind=kOutput, calls=%fused_computation.105 | convolution fusion | flops 905969664 | bytes 10747904 | tf_op jit(solution)/shard_map/dot_general | solution.py:119
  218.9 3.1 convolution_bitcast_fusion
  222.0 0.7 slice_bitcast_fusion.3
  224.3 0.7 slice_bitcast_fusion.6
  228.8 3.1 copy.39
  231.9 3.5 reshape.271
  235.4 1.3 slice.183
  236.7 1.5 collective-permute-start.1
  238.2 1.9 slice_bitcast_fusion.7
  240.2 3.9 convolution_convert_fusion
  244.0 1.2 fusion.39
  245.3 1.3 fusion.41
  247.1 13.6 %all-reduce.10 = (f32[32]{0:T(128)S(1)}, f32[32]{0:T(128)S(1)}) all-reduce(f32[32]{0:T(128)S(1)} %reduce_sum.75, f32[32]{0:T(128)S(1)} %reduce_sum.72), channel_id=1, replica_groups=mesh['dp'=8,'tm'=4] {'tm'}, use_global_device_ids=true, to_apply=%region_11.12 | all-reduce | flops 64 | bytes 512 | tf_op jit(solution)/shard_map/psum | solution.py:107
  261.0 92.3 %reduce-scatter.2.cloned.1.call-done = f32[864,256]{1,0:T(8,128)} async-done(((f32[6912,256]{1,0:T(8,128)}), f32[864,256]{1,0:T(8,128)}) %reduce-scatter.2.cloned.1.call-update) | async-done | bytes 884752 | tf_op jit(solution)/shard_map/reduce_scatter | solution.py:123
  353.3 1.6 fusion.37
  354.9 35.1 %all-reduce.14.cloned.1.call-done = f32[864,256]{1,0:T(8,128)} async-done(((f32[864,256]{1,0:T(8,128)}), f32[864,256]{1,0:T(8,128)}) %all-reduce.14.cloned.1.call-update) | async-done | bytes 884752 | tf_op jit(solution)/shard_map/psum | solution.py:122
  390.0 2.1 copy.76
  (80 shorter events, 7.5 us)
Async XLA Ops:
  7.2 205.4 %copy-start = (bf16[1,4,8,8,256]{4,3,2,1,0:T(8,128)(2,1)S(1)}, bf16[1,4,8,8,256]{4,3,2,1,0:T(8,128)(2,1)}, u32[]{:S(2)}) copy-start(bf16[1,4,8,8,256]{4,3,2,1,0:T(8,128)(2,1)} %param.11) | copy-start | bytes 393220
  7.2 211.7 %all-gather.2.cloned.1.call-start = ((), (), s32[]{:S(2)}) async-start(), calls=%async_computation.1 | async-start | bytes 3981312 | tf_op jit(solution)/shard_map/all_gather | solution.py:95
  7.9 345.4 %reduce-scatter.2.cloned.1.call-start = ((), (), s32[]{:S(2)}) async-start(), calls=%async_computation.2 | async-start | bytes 7962624 | tf_op jit(solution)/shard_map/reduce_scatter | solution.py:123
  21.7 2.4 collective-permute-start
  201.1 11.1 %copy-start.9 = (bf16[4,8,8,256]{3,2,1,0:T(8,128)(2,1)S(1)}, bf16[4,8,8,256]{3,2,1,0:T(8,128)(2,1)}, u32[]{:S(2)}) copy-start(bf16[4,8,8,256]{3,2,1,0:T(8,128)(2,1)} %slice.142) | copy-start | bytes 393220
  201.1 11.2 %copy-start.8 = (bf16[4,8,8,256]{3,2,1,0:T(8,128)(2,1)S(1)}, bf16[4,8,8,256]{3,2,1,0:T(8,128)(2,1)}, u32[]{:S(2)}) copy-start(bf16[4,8,8,256]{3,2,1,0:T(8,128)(2,1)} %slice.143) | copy-start | bytes 393220
  201.1 11.2 %copy-start.7 = (bf16[4,8,8,256]{3,2,1,0:T(8,128)(2,1)S(1)}, bf16[4,8,8,256]{3,2,1,0:T(8,128)(2,1)}, u32[]{:S(2)}) copy-start(bf16[4,8,8,256]{3,2,1,0:T(8,128)(2,1)} %slice.144) | copy-start | bytes 393220
  201.1 11.2 %copy-start.6 = (bf16[4,8,8,256]{3,2,1,0:T(8,128)(2,1)S(1)}, bf16[4,8,8,256]{3,2,1,0:T(8,128)(2,1)}, u32[]{:S(2)}) copy-start(bf16[4,8,8,256]{3,2,1,0:T(8,128)(2,1)} %slice.145) | copy-start | bytes 393220
  201.1 11.2 %copy-start.5 = (bf16[4,8,8,256]{3,2,1,0:T(8,128)(2,1)S(1)}, bf16[4,8,8,256]{3,2,1,0:T(8,128)(2,1)}, u32[]{:S(2)}) copy-start(bf16[4,8,8,256]{3,2,1,0:T(8,128)(2,1)} %slice.146) | copy-start | bytes 393220
  212.5 1.8 copy-start.3
  218.4 171.6 %all-reduce.14.cloned.1.call-start = ((), (), s32[]{:S(2)}) async-start(), calls=%async_computation.3 | async-start | bytes 1769472 | tf_op jit(solution)/shard_map/psum | solution.py:122
  235.4 4.8 %copy-start.4 = (bf16[256,6912]{1,0:T(8,128)(2,1)S(1)}, bf16[256,6912]{1,0:T(8,128)(2,1)}, u32[]{:S(2)}) copy-start(bf16[256,6912]{1,0:T(8,128)(2,1)} %copy-done.3) | copy-start | bytes 10616836
  236.7 7.3 %collective-permute-start.1 = (f32[2,16,16,256]{3,2,1,0:T(8,128)S(1)}, f32[2,16,16,256]{3,2,1,0:T(8,128)S(1)}, u32[]{:S(2)}, u32[]{:S(2)}) collective-permute-start(f32[2,16,16,256]{3,2,1,0:T(8,128)S(1)} %slice.183), channel_id=1, source_target_pairs={{1,0},{2,1},{3,2},{5,4},{6,5},{7,6},{9,8},{10,9},{11,10},{13,12},{... | collective-permute-start | bytes 1572872 | tf_op jit(solution)/shard_map/ppermute | solution.py:13
  240.2 5.1 %copy-start.2 = (bf16[1,8,16,16,256]{4,3,2,1,0:T(8,128)(2,1)S(1)}, bf16[1,8,16,16,256]{4,3,2,1,0:T(8,128)(2,1)}, u32[]{:S(2)}) copy-start(bf16[1,8,16,16,256]{4,3,2,1,0:T(8,128)(2,1)} %param.6) | copy-start | bytes 3145732
  240.2 5.1 %copy-start.10 = (f32[256]{0:T(256)S(1)}, f32[256]{0:T(256)}, u32[]{:S(2)}) copy-start(f32[256]{0:T(256)} %param.10) | copy-start | bytes 3076
  240.2 5.1 %copy-start.11 = (f32[256]{0:T(256)S(1)}, f32[256]{0:T(256)}, u32[]{:S(2)}) copy-start(f32[256]{0:T(256)} %param.9) | copy-start | bytes 3076
  353.3 38.8 %copy-start.1 = (bf16[1,4,8,8,256]{4,3,2,1,0:T(8,128)(2,1)S(1)}, bf16[1,4,8,8,256]{4,3,2,1,0:T(8,128)(2,1)}, u32[]{:S(2)}) copy-start(bf16[1,4,8,8,256]{4,3,2,1,0:T(8,128)(2,1)} %param.11) | copy-start | bytes 393220
Sparse Core Ops, SparseCore 0:
  10.2 67.8 all-gather.1
  218.5 134.7 reduce-scatter.1
  355.8 34.1 all-reduce.13
where the time goes:
time: 399 us
  local copies, waits for them, and re-layouts  206 us (52%)
  waiting for transfers between devices  129 us (32%)
  blocking collectives  21.9 us (5%)
  between operations  15.1 us (4%)
  other arithmetic  12.5 us (3%)
  matrix products  11 us (3%)
    slice x27, local copies, waits for them, and re-layouts, unfold(): padded[step_t:step_t + 2 * frames_out:2, step_r:step_r + 2 * rows_out:2,...  176 us
    reduce_scatter x1, waiting for transfers between devices, shards(): lax.psum_scatter(clip_grad, 'dp', scatter_dimension=0, tiled=True)  92.3 us
    psum x1, waiting for transfers between devices, shards(): clip_grad = lax.psum(local_grad, 'tm')  35.1 us
    unnamed x51, local copies, waits for them, and re-layouts  15.1 us
    psum x1, blocking collectives, shards(): lax.psum((jnp.sum(grad_norm, axis=(0, 1, 2, 4)), jnp.sum(grad_norm * norm...  13.6 us
    psum x1, blocking collectives, shards(): lax.psum((jnp.sum(values * mask_group, axis=(0, 1, 2, 4)), jnp.sum(values...  8.37 us
  transfers between devices with their start and end apart: 5, of which 3 were waited for; matrix products, arithmetic and copies ran while one was open for 57% of the time, Pallas kernels for 0%

commit v1 on v0

--- a/solution.py
+++ b/solution.py
@@ -5,6 +5,15 @@
 
 GROUPS = 32
 EPS = 1e-06
+
+
+def doubling_sum(x, mesh_axis):
+    peers = lax.axis_size(mesh_axis)
+    summed, hop = (x, 1)
+    while hop < peers:
+        summed = summed + lax.ppermute(summed, mesh_axis, [(i, i ^ hop) for i in range(peers)])
+        hop = 2 * hop
+    return summed
 
 
 def shifted(value, axis, by):
@@ -119,7 +128,7 @@
     local_grad = lax.dot_general(
         patches, cot_rows, (((0,), (0,)), ((), ())), preferred_element_type=jnp.float32
     )
-    clip_grad = lax.psum(local_grad, "tm")
+    clip_grad = doubling_sum(local_grad, "tm")
     weight_grad = lax.psum_scatter(clip_grad, "dp", scatter_dimension=0, tiled=True)
     return (out_block[None], input_grad[None], weight_grad)
 

time: 399 us -> 536 us (1.34)
  waiting for transfers between devices: 129 us -> 255 us
  other arithmetic: 12.5 us -> 25.2 us
  starting transfers between devices: 3.12 us -> 9.07 us
    ppermute x0 -> x2, waiting for transfers between devices: none -> 164 us  [doubling_sum(): lax.ppermute(summed, mesh_axis, [(i, i ^ hop) for i in range(peers)])]
    psum x1 -> x0, waiting for transfers between devices: 35.1 us -> none  [shards(): clip_grad = lax.psum(local_grad, 'tm')]
    add x0 -> x2, other arithmetic: none -> 12.7 us  [doubling_sum(): summed + lax.ppermute(summed, mesh_axis, [(i, i ^ hop) for i in range(pee...]
    ppermute x0 -> x2, starting transfers between devices: none -> 5.99 us  [doubling_sum(): lax.ppermute(summed, mesh_axis, [(i, i ^ hop) for i in range(peers)])]
    unnamed x51 -> x46, local copies, waits for them, and re-layouts: 15.1 us -> 13.6 us
  transfers between devices with their start and end apart: 5 -> 6, of which waited for: 3 -> 4; matrix products, arithmetic and copies ran while one was open for 57% -> 7% of each run, Pallas kernels for 0% -> 0%
where the time goes in v1:
time: 536 us; the launch traced here: 535 us
  waiting for transfers between devices  255 us (48%)
  local copies, waits for them, and re-layouts  204 us (38%)
  other arithmetic  25.2 us (5%)
  blocking collectives  18.1 us (3%)
  between operations  15.3 us (3%)
  starting transfers between devices  9.07 us (2%)
  matrix products  8.11 us (2%)
    slice x27, local copies, waits for them, and re-layouts, unfold(): padded[step_t:step_t + 2 * frames_out:2, step_r:step_r + 2 * rows_out:2,...  176 us
    ppermute x2, waiting for transfers between devices, doubling_sum(): lax.ppermute(summed, mesh_axis, [(i, i ^ hop) for i in range(peers)])  164 us
    reduce_scatter x1, waiting for transfers between devices, shards(): lax.psum_scatter(clip_grad, 'dp', scatter_dimension=0, tiled=True)  90.6 us
    unnamed x46, local copies, waits for them, and re-layouts  13.6 us
    add x2, other arithmetic, doubling_sum(): summed + lax.ppermute(summed, mesh_axis, [(i, i ^ hop) for i in range(pee...  12.7 us
  transfers between devices with their start and end apart: 6, of which 4 were waited for; matrix products, arithmetic and copies ran while one was open for 7% of the time, Pallas kernels for 0%

profile of v1, /device:TPU:0, one launch (start us, length us, event | category | flops | bytes accessed | tf_op | source)
XLA Modules:
  0.0 535.4 jit_solution(13937076589340626032)
XLA Ops:
  7.9 1.8 fusion.18
  10.2 8.4 %all-reduce.11 = (f32[32]{0:T(128)S(1)}, f32[32]{0:T(128)S(1)}) all-reduce(f32[32]{0:T(128)S(1)} %reduce_sum.51, f32[32]{0:T(128)S(1)} %reduce_sum.54), channel_id=1, replica_groups=mesh['dp'=8,'tm'=4] {'tm'}, use_global_device_ids=true, to_apply=%region_2.0 | all-reduce | flops 64 | bytes 512 | tf_op jit(solution)/shard_map/psum | solution.py:85
  18.9 2.0 fusion.15
  21.0 1.3 collective-permute-start
  22.3 1.1 collective-permute-done
  23.4 1.0 fusion.38
  24.4 9.8 %slice.130 = bf16[4,8,8,256]{3,2,1,0:T(8,128)(2,1)} slice(bf16[10,17,17,256]{3,2,1,0:T(8,128)(2,1)S(1)} %fusion.38), slice={[0:8:2], [0:16:2], [0:16:2], [0:256:1]} | slice | bytes 262144 | tf_op jit(solution)/shard_map/slice | solution.py:30
  34.2 9.7 %slice.131 = bf16[4,8,8,256]{3,2,1,0:T(8,128)(2,1)} slice(bf16[10,17,17,256]{3,2,1,0:T(8,128)(2,1)S(1)} %fusion.38), slice={[0:8:2], [0:16:2], [1:17:2], [0:256:1]} | slice | bytes 262144 | tf_op jit(solution)/shard_map/slice | solution.py:30
  44.0 9.8 %slice.132 = bf16[4,8,8,256]{3,2,1,0:T(8,128)(2,1)} slice(bf16[10,17,17,256]{3,2,1,0:T(8,128)(2,1)S(1)} %fusion.38), slice={[0:8:2], [0:16:2], [2:17:2], [0:256:1]} | slice | bytes 262144 | tf_op jit(solution)/shard_map/slice | solution.py:30
  53.7 9.7 %slice.133 = bf16[4,8,8,256]{3,2,1,0:T(8,128)(2,1)} slice(bf16[10,17,17,256]{3,2,1,0:T(8,128)(2,1)S(1)} %fusion.38), slice={[0:8:2], [1:17:2], [0:16:2], [0:256:1]} | slice | bytes 262144 | tf_op jit(solution)/shard_map/slice | solution.py:30
  63.5 9.7 %slice.134 = bf16[4,8,8,256]{3,2,1,0:T(8,128)(2,1)} slice(bf16[10,17,17,256]{3,2,1,0:T(8,128)(2,1)S(1)} %fusion.38), slice={[0:8:2], [1:17:2], [1:17:2], [0:256:1]} | slice | bytes 262144 | tf_op jit(solution)/shard_map/slice | solution.py:30
  73.2 9.8 %slice.135 = bf16[4,8,8,256]{3,2,1,0:T(8,128)(2,1)} slice(bf16[10,17,17,256]{3,2,1,0:T(8,128)(2,1)S(1)} %fusion.38), slice={[0:8:2], [1:17:2], [2:17:2], [0:256:1]} | slice | bytes 262144 | tf_op jit(solution)/shard_map/slice | solution.py:30
  82.9 9.7 %slice.136 = bf16[4,8,8,256]{3,2,1,0:T(8,128)(2,1)} slice(bf16[10,17,17,256]{3,2,1,0:T(8,128)(2,1)S(1)} %fusion.38), slice={[0:8:2], [2:17:2], [0:16:2], [0:256:1]} | slice | bytes 262144 | tf_op jit(solution)/shard_map/slice | solution.py:30
  92.6 9.7 %slice.137 = bf16[4,8,8,256]{3,2,1,0:T(8,128)(2,1)} slice(bf16[10,17,17,256]{3,2,1,0:T(8,128)(2,1)S(1)} %fusion.38), slice={[0:8:2], [2:17:2], [1:17:2], [0:256:1]} | slice | bytes 262144 | tf_op jit(solution)/shard_map/slice | solution.py:30
  102.4 9.7 %slice.138 = bf16[4,8,8,256]{3,2,1,0:T(8,128)(2,1)} slice(bf16[10,17,17,256]{3,2,1,0:T(8,128)(2,1)S(1)} %fusion.38), slice={[0:8:2], [2:17:2], [2:17:2], [0:256:1]} | slice | bytes 262144 | tf_op jit(solution)/shard_map/slice | solution.py:30
  112.1 9.7 %slice.139 = bf16[4,8,8,256]{3,2,1,0:T(8,128)(2,1)} slice(bf16[10,17,17,256]{3,2,1,0:T(8,128)(2,1)S(1)} %fusion.38), slice={[1:9:2], [0:16:2], [0:16:2], [0:256:1]} | slice | bytes 262144 | tf_op jit(solution)/shard_map/slice | solution.py:30
  121.8 9.7 %slice.140 = bf16[4,8,8,256]{3,2,1,0:T(8,128)(2,1)} slice(bf16[10,17,17,256]{3,2,1,0:T(8,128)(2,1)S(1)} %fusion.38), slice={[1:9:2], [0:16:2], [1:17:2], [0:256:1]} | slice | bytes 262144 | tf_op jit(solution)/shard_map/slice | solution.py:30
  131.5 9.7 %slice.141 = bf16[4,8,8,256]{3,2,1,0:T(8,128)(2,1)} slice(bf16[10,17,17,256]{3,2,1,0:T(8,128)(2,1)S(1)} %fusion.38), slice={[1:9:2], [0:16:2], [2:17:2], [0:256:1]} | slice | bytes 262144 | tf_op jit(solution)/shard_map/slice | solution.py:30
  141.3 9.7 %slice.142 = bf16[4,8,8,256]{3,2,1,0:T(8,128)(2,1)} slice(bf16[10,17,17,256]{3,2,1,0:T(8,128)(2,1)S(1)} %fusion.38), slice={[1:9:2], [1:17:2], [0:16:2], [0:256:1]} | slice | bytes 262144 | tf_op jit(solution)/shard_map/slice | solution.py:30
  151.0 9.7 %slice.143 = bf16[4,8,8,256]{3,2,1,0:T(8,128)(2,1)} slice(bf16[10,17,17,256]{3,2,1,0:T(8,128)(2,1)S(1)} %fusion.38), slice={[1:9:2], [1:17:2], [1:17:2], [0:256:1]} | slice | bytes 262144 | tf_op jit(solution)/shard_map/slice | solution.py:30
  160.7 9.8 %slice.144 = bf16[4,8,8,256]{3,2,1,0:T(8,128)(2,1)} slice(bf16[10,17,17,256]{3,2,1,0:T(8,128)(2,1)S(1)} %fusion.38), slice={[1:9:2], [1:17:2], [2:17:2], [0:256:1]} | slice | bytes 262144 | tf_op jit(solution)/shard_map/slice | solution.py:30
  170.5 9.7 %slice.145 = bf16[4,8,8,256]{3,2,1,0:T(8,128)(2,1)} slice(bf16[10,17,17,256]{3,2,1,0:T(8,128)(2,1)S(1)} %fusion.38), slice={[1:9:2], [2:17:2], [0:16:2], [0:256:1]} | slice | bytes 262144 | tf_op jit(solution)/shard_map/slice | solution.py:30
  180.2 9.7 %slice.146 = bf16[4,8,8,256]{3,2,1,0:T(8,128)(2,1)} slice(bf16[10,17,17,256]{3,2,1,0:T(8,128)(2,1)S(1)} %fusion.38), slice={[1:9:2], [2:17:2], [1:17:2], [0:256:1]} | slice | bytes 262144 | tf_op jit(solution)/shard_map/slice | solution.py:30
  189.9 1.5 slice.147
  192.9 0.9 slice.150
  193.8 0.8 slice.151
  194.6 0.8 slice.152
  195.4 0.9 slice.153
  196.3 1.2 slice.154
  197.5 1.2 slice.155
  198.7 1.5 slice.156
  200.3 1.0 constant_dynamic-update-slice_fusion.26
  201.2 0.9 constant_dynamic-update-slice_fusion.25
  202.2 0.9 constant_dynamic-update-slice_fusion.24
  203.1 0.9 constant_dynamic-update-slice_fusion.23
  204.0 0.9 constant_dynamic-update-slice_fusion.22
  204.9 0.9 constant_dynamic-update-slice_fusion.21
  205.8 0.9 constant_dynamic-update-slice_fusion.20
  206.8 0.9 constant_dynamic-update-slice_fusion.19
  207.7 0.9 constant_dynamic-update-slice_fusion.18
  208.6 0.9 constant_dynamic-update-slice_fusion.17
  209.5 0.9 constant_dynamic-update-slice_fusion.16
  210.4 0.9 constant_dynamic-update-slice_fusion.15
  211.3 0.9 constant_dynamic-update-slice_fusion.14
  212.3 0.9 constant_dynamic-update-slice_fusion.13
  213.5 1.1 fusion.43
  215.2 3.2 collective-permute-start.2
  218.5 10.9 %collective-permute-done.2 = f32[6912,256]{1,0:T(8,128)S(1)} collective-permute-done((f32[6912,256]{1,0:T(8,128)S(1)}, f32[6912,256]{1,0:T(8,128)S(1)}, u32[]{:S(2)}, u32[]{:S(2)}) %collective-permute-start.2) | collective-permute-done | bytes 7077920 | tf_op jit(solution)/shard_map/ppermute | solution.py:14
  229.4 3.8 add.118
  233.2 2.7 collective-permute-start.3
  236.2 152.7 %collective-permute-done.3 = f32[6912,256]{1,0:T(8,128)} collective-permute-done((f32[6912,256]{1,0:T(8,128)}, f32[6912,256]{1,0:T(8,128)}, u32[]{:S(2)}, u32[]{:S(2)}) %collective-permute-start.3) | collective-permute-done | bytes 7077920 | tf_op jit(solution)/shard_map/ppermute | solution.py:14
  388.9 8.9 %add.119 = f32[6912,256]{1,0:T(8,128)} add(f32[6912,256]{1,0:T(8,128)} %add.118, f32[6912,256]{1,0:T(8,128)} %collective-permute-done.3) | non-fusion elementwise | flops 1769472 | bytes 21233664 | tf_op jit(solution)/shard_map/add | solution.py:14
  398.2 3.1 convolution_bitcast_fusion
  408.0 3.1 copy.39
  411.1 3.5 reshape.271
  414.6 1.3 slice.183
  415.9 1.5 collective-permute-start.1
  417.5 1.9 slice_bitcast_fusion.7
  419.4 3.8 convolution_convert_fusion
  423.3 1.3 fusion.39
  424.6 1.3 fusion.41
  426.3 9.8 %all-reduce.10 = (f32[32]{0:T(128)S(1)}, f32[32]{0:T(128)S(1)}) all-reduce(f32[32]{0:T(128)S(1)} %reduce_sum.75, f32[32]{0:T(128)S(1)} %reduce_sum.72), channel_id=1, replica_groups=mesh['dp'=8,'tm'=4] {'tm'}, use_global_device_ids=true, to_apply=%region_11.12 | all-reduce | flops 64 | bytes 512 | tf_op jit(solution)/shard_map/psum | solution.py:116
  436.4 1.6 fusion.37
  438.0 90.6 %reduce-scatter.2.cloned.1.call-done = f32[864,256]{1,0:T(8,128)} async-done(((f32[6912,256]{1,0:T(8,128)}), f32[864,256]{1,0:T(8,128)}) %reduce-scatter.2.cloned.1.call-update) | async-done | bytes 884752 | tf_op jit(solution)/shard_map/reduce_scatter | solution.py:132
  (78 shorter events, 11.1 us)
Async XLA Ops:
  7.2 206.3 %copy-start = (bf16[1,4,8,8,256]{4,3,2,1,0:T(8,128)(2,1)S(1)}, bf16[1,4,8,8,256]{4,3,2,1,0:T(8,128)(2,1)}, u32[]{:S(2)}) copy-start(bf16[1,4,8,8,256]{4,3,2,1,0:T(8,128)(2,1)} %param.11) | copy-start | bytes 393220
  7.2 391.0 %all-gather.2.cloned.1.call-start = ((), (), s32[]{:S(2)}) async-start(), calls=%async_computation.1 | async-start | bytes 3981312 | tf_op jit(solution)/shard_map/all_gather | solution.py:104
  21.0 2.4 collective-permute-start
  200.3 12.9 %copy-start.7 = (bf16[4,8,8,256]{3,2,1,0:T(8,128)(2,1)S(1)}, bf16[4,8,8,256]{3,2,1,0:T(8,128)(2,1)}, u32[]{:S(2)}) copy-start(bf16[4,8,8,256]{3,2,1,0:T(8,128)(2,1)} %slice.144) | copy-start | bytes 393220
  200.3 13.0 %copy-start.6 = (bf16[4,8,8,256]{3,2,1,0:T(8,128)(2,1)S(1)}, bf16[4,8,8,256]{3,2,1,0:T(8,128)(2,1)}, u32[]{:S(2)}) copy-start(bf16[4,8,8,256]{3,2,1,0:T(8,128)(2,1)} %slice.145) | copy-start | bytes 393220
  200.3 13.0 %copy-start.5 = (bf16[4,8,8,256]{3,2,1,0:T(8,128)(2,1)S(1)}, bf16[4,8,8,256]{3,2,1,0:T(8,128)(2,1)}, u32[]{:S(2)}) copy-start(bf16[4,8,8,256]{3,2,1,0:T(8,128)(2,1)} %slice.146) | copy-start | bytes 393220
  213.5 1.7 copy-start.3
  215.2 14.2 %collective-permute-start.2 = (f32[6912,256]{1,0:T(8,128)S(1)}, f32[6912,256]{1,0:T(8,128)S(1)}, u32[]{:S(2)}, u32[]{:S(2)}) collective-permute-start(f32[6912,256]{1,0:T(8,128)S(1)} %fusion.43), channel_id=1, source_target_pairs={{0,1},{1,0},{2,3},{3,2},{4,5},{5,4},{6,7},{7,6},{8,9},{9,8},{10,11... | collective-permute-start | bytes 21233672 | tf_op jit(solution)/shard_map/ppermute | solution.py:14
  233.2 155.7 %collective-permute-start.3 = (f32[6912,256]{1,0:T(8,128)}, f32[6912,256]{1,0:T(8,128)}, u32[]{:S(2)}, u32[]{:S(2)}) collective-permute-start(f32[6912,256]{1,0:T(8,128)} %add.118), channel_id=1, source_target_pairs={{0,2},{1,3},{2,0},{3,1},{4,6},{5,7},{6,4},{7,5},{8,10},{9,11},{10,... | collective-permute-start | bytes 21233672 | tf_op jit(solution)/shard_map/ppermute | solution.py:14
  236.0 292.6 %reduce-scatter.2.cloned.1.call-start = ((), (), s32[]{:S(2)}) async-start(), calls=%async_computation.2 | async-start | bytes 7962624 | tf_op jit(solution)/shard_map/reduce_scatter | solution.py:132
  414.6 4.8 copy-start.4
  415.9 7.3 %collective-permute-start.1 = (f32[2,16,16,256]{3,2,1,0:T(8,128)S(1)}, f32[2,16,16,256]{3,2,1,0:T(8,128)S(1)}, u32[]{:S(2)}, u32[]{:S(2)}) collective-permute-start(f32[2,16,16,256]{3,2,1,0:T(8,128)S(1)} %slice.183), channel_id=1, source_target_pairs={{1,0},{2,1},{3,2},{5,4},{6,5},{7,6},{9,8},{10,9},{11,10},{13,12},{... | collective-permute-start | bytes 1572872 | tf_op jit(solution)/shard_map/ppermute | solution.py:22
  419.4 5.2 copy-start.2
  419.4 5.2 copy-start.8
  419.4 5.2 copy-start.9
  423.3 105.3 %copy-start.1 = (bf16[1,4,8,8,256]{4,3,2,1,0:T(8,128)(2,1)S(1)}, bf16[1,4,8,8,256]{4,3,2,1,0:T(8,128)(2,1)}, u32[]{:S(2)}) copy-start(bf16[1,4,8,8,256]{4,3,2,1,0:T(8,128)(2,1)} %param.11) | copy-start | bytes 393220
Sparse Core Ops, SparseCore 0:
  236.1 65.5 all-gather.1
  398.0 130.5 reduce-scatter.1
